TPU v7x, 32 devices: a whole 2x2x4 slice. The times are simulated.
32 devices in a mesh: gx: 8 (over y, x, core), gy: 4 (over z).
Axes of the slice: x: 2, y: 2, z: 4, core: 2. Of those that a mesh axis runs over, the one named last changes fastest.
Arguments:
- basis: float32 [32, 64, 32, 256], P(None, 'gx', 'gy'), may hold values from -6 to 6
- rhs: float32 [64, 32, 256], P('gx', 'gy'), may hold values from -12 to 12
- extra_diag: float32 [64, 32, 256], P('gx', 'gy'), may hold values from 0.02 to 0.5
- coeff: float32 [3, 64, 32, 256], P(None, 'gx', 'gy'), may hold values from 0.3 to 3
Outputs:
- guess: float32 [64, 32, 256], P('gx', 'gy')
- stepped: float32 [64, 32, 256], P('gx', 'gy')
All inputs are finite; a program needn't handle non-finite values.
Results may differ from a plain program's by a relative error of at most 0.0003.
Values sent between devices are 32-bit elements; how exact they have to be, the bound alone decides.
No kernel may reach another device: no remote copies, remote signals or barrier semaphores. Data moves between devices by JAX's collectives and lax.ppermute only.
A program may use at most 64 MiB of HBM per device.

v0:
```python
import jax
import jax.numpy as jnp
from jax import lax
from jax.sharding import PartitionSpec as P

precise = lax.Precision.HIGHEST


def shifted(block, axis, distance):
    devices = range(lax.axis_size(axis))
    route = [(i - distance, i) for i in devices if i - distance in devices]
    return lax.ppermute(block, axis, route)


def padded_2(cells, sides, width):
    for axis, dim in sides:
        count = lax.axis_size(axis)
        ends = count - 1
        head = lax.slice_in_dim(cells, 0, width, axis=dim)
        tail = lax.slice_in_dim(cells, cells.shape[dim] - width, cells.shape[dim], axis=dim)
        cells = jnp.concatenate(
            [
                lax.ppermute(tail, axis, [(i, (i + 1) % count) for i in range(ends)]),
                cells,
                lax.ppermute(head, axis, [((i + 1) % count, i) for i in range(ends)]),
            ],
            axis=dim,
        )
    return cells


def flux_apply(padded, coeff_pad, extra):
    center = padded[:, 1:-1, 1:-1]
    coeff_mid = coeff_pad[:, 1:-1, 1:-1]
    flux_x = coeff_mid[0] * (center - padded[:, 2:, 1:-1])
    flux_y = coeff_mid[1] * (center - padded[:, 1:-1, 2:])
    below_x = coeff_pad[0, :-2, 1:-1] * (padded[:, :-2, 1:-1] - center)
    below_y = coeff_pad[1, 1:-1, :-2] * (padded[:, 1:-1, :-2] - center)
    next_z = jnp.concatenate([center[..., 1:], jnp.zeros_like(center[..., :1])], axis=-1)
    flux_z = coeff_mid[2] * (center - next_z)
    below_z = jnp.concatenate([jnp.zeros_like(flux_z[..., :1]), flux_z[..., :-1]], axis=-1)
    return extra * center + flux_x + flux_y + flux_z - below_x - below_y - below_z


def small_solve(matrix, vector):
    lower = jnp.linalg.cholesky(matrix)
    middle = lax.linalg.triangular_solve(lower, vector[:, None], left_side=True, lower=True)
    result = lax.linalg.triangular_solve(
        lower, middle, left_side=True, lower=True, transpose_a=True
    )
    return result[:, 0]


def on_device(basis, rhs, extra_diag, coeff):
    lower_x = shifted(coeff[0][-1:], "gx", 1)
    lower_y = shifted(coeff[1][:, -1:], "gy", 1)
    coeff_pad = jnp.pad(coeff, ((0, 0), (1, 1), (1, 1), (0, 0)))
    coeff_pad = coeff_pad.at[0, 0, 1:-1].set(lower_x[0])
    coeff_pad = coeff_pad.at[1, 1:-1, 0].set(lower_y[:, 0])
    count = basis.shape[0]
    flat_basis = basis.reshape(count, -1)
    padded_basis = padded_2(basis, (("gx", 1), ("gy", 2)), 1)
    applied = flux_apply(padded_basis, coeff_pad, extra_diag)
    local_gram = jnp.dot(flat_basis, applied.reshape(count, -1).T, precision=precise)
    local_proj = jnp.dot(flat_basis, rhs.reshape(-1), precision=precise)
    gram, projected = lax.psum((local_gram, local_proj), ("gx", "gy"))
    gram = 0.5 * (gram + gram.T)
    weights = small_solve(gram, projected)
    guess = jnp.tensordot(weights, basis, axes=1, precision=precise)
    residual = rhs - jnp.tensordot(weights, applied, axes=1, precision=precise)
    coeff_mid = coeff_pad[:, 1:-1, 1:-1]
    below_kz = jnp.concatenate([jnp.zeros_like(coeff[2][..., :1]), coeff[2][..., :-1]], axis=-1)
    diagonal = (
        extra_diag
        + coeff_mid[0]
        + coeff_mid[1]
        + coeff_mid[2]
        + coeff_pad[0, :-2, 1:-1]
        + coeff_pad[1, 1:-1, :-2]
        + below_kz
    )
    direction = residual / diagonal
    direction_pad = padded_2(direction, (("gx", 0), ("gy", 1)), 1)
    applied_dir = flux_apply(direction_pad[None], coeff_pad, extra_diag)[0]
    local_corr = jnp.dot(flat_basis, applied_dir.reshape(-1), precision=precise)
    correction, numerator, curvature = lax.psum(
        (local_corr, jnp.sum(residual * direction), jnp.sum(direction * applied_dir)), ("gx", "gy")
    )
    shift_coef = small_solve(gram, correction)
    update = direction - jnp.tensordot(shift_coef, basis, axes=1, precision=precise)
    denominator = curvature - jnp.dot(correction, shift_coef, precision=precise)
    step_size = numerator / denominator
    return (guess, guess + step_size * update)


def solution(mesh):
    placed = (
        P(None, "gx", "gy", None),
        P("gx", "gy", None),
        P("gx", "gy", None),
        P(None, "gx", "gy", None),
    )
    return jax.shard_map(
        on_device,
        mesh=mesh,
        in_specs=placed,
        out_specs=(P("gx", "gy", None), P("gx", "gy", None)),
        check_vma=False,
    )
```

profile of v0, /device:TPU:0, one launch (start us, length us, event | category | flops | bytes accessed | tf_op | source)
XLA Modules:
  0.0 160.6 jit_solution(4980887315087795019)
XLA Ops:
  1.3 2.5 %collective-permute-start = (f32[1,8,256]{2,1,0:T(8,128)S(1)}, f32[1,8,256]{2,1,0:T(8,128)S(1)}, u32[]{:S(2)}, u32[]{:S(2)}) collective-permute-start(f32[1,8,256]{2,1,0:T(8,128)S(1)} %slice_bitcast_fusion.7), channel_id=1, source_target_pairs={{0,4},{4,8},{8,12},{12,16},{16,20},{20,24},{24,28},{1,5},{5,9},{9,... | collective-permute-start | bytes 24584 | tf_op jit(solution)/shard_map/ppermute | solution.py:12
  3.9 2.8 %copy.11 = f32[32,8,8,256]{3,0,2,1:T(8,128)S(1)} copy(f32[32,8,8,256]{3,2,1,0:T(8,128)} %param.13) | data formatting | bytes 4194304 | tf_op args[0]
  7.6 4.5 %collective-permute-start.3 = (f32[32,1,8,256]{3,0,2,1:T(8,128)}, f32[32,1,8,256]{3,0,2,1:T(8,128)S(1)}, u32[]{:S(2)}, u32[]{:S(2)}) collective-permute-start(f32[32,1,8,256]{3,0,2,1:T(8,128)} %get-tuple-element.44), channel_id=1, source_target_pairs={{0,4},{4,8},{8,12},{12,16},{16,20},{20,24},{24,28},{1,5},{5,9},{9,... | collective-permute-start | bytes 786440 | tf_op jit(solution)/shard_map/ppermute | solution.py:23
  12.1 3.5 %collective-permute-start.1 = (f32[8,1,256]{2,1,0:T(1,128)S(1)}, f32[8,1,256]{2,1,0:T(1,128)S(1)}, u32[]{:S(2)}, u32[]{:S(2)}) collective-permute-start(f32[8,1,256]{2,1,0:T(1,128)S(1)} %slice.229), channel_id=1, source_target_pairs={{0,1},{1,2},{2,3},{4,5},{5,6},{6,7},{8,9},{9,10},{10,11},{12,13},{... | collective-permute-start | bytes 24584 | tf_op jit(solution)/shard_map/ppermute | solution.py:12
  15.6 1.4 collective-permute-start.2
  17.1 1.9 %slice.236 = f32[32,8,8,255]{3,0,2,1:T(8,128)} slice(f32[32,8,8,256]{3,0,2,1:T(8,128)S(1)} %copy.11), slice={[0:32], [0:8], [0:8], [1:256]} | slice | bytes 4177920 | tf_op jit(solution)/shard_map/slice | solution.py:39
  19.4 3.0 %subtract_multiply_fusion = (f32[32,8,8,256]{3,0,2,1:T(8,128)S(1)}, f32[32,10,8,256]{3,0,2,1:T(8,128)S(1)}) fusion(f32[32,8,8,255]{3,0,2,1:T(8,128)} %slice.236, f32[8,8,256]{2,1,0:T(8,128)S(1)} %get-tuple-element.48, f32[32,8,8,256]{3,2,1,0:T(8,128)S(1)} %copy-done, f32[32,10,8,256]{3,0,2,1:T(8,128)S(1)} %constant_dynamic-update-slice_fusion.2), kind=kLoop, calls=%fused_computation.18 | loop fusion | flops 1048576 | bytes 8445952 | tf_op jit(solution)/shard_map/mul | solution.py:40
  24.0 4.6 %collective-permute-start.5 = (f32[32,10,1,256]{3,0,2,1:T(8,128)S(1)}, f32[32,10,1,256]{3,0,2,1:T(8,128)S(1)}, u32[]{:S(2)}, u32[]{:S(2)}) collective-permute-start(f32[32,10,1,256]{3,0,2,1:T(8,128)S(1)} %get-tuple-element.40), channel_id=1, source_target_pairs={{0,1},{1,2},{2,3},{4,5},{5,6},{6,7},{8,9},{9,10},{10,11},{12,13},{... | collective-permute-start | bytes 983048 | tf_op jit(solution)/shard_map/ppermute | solution.py:23
  28.5 2.8 %convolution_bitcast_fusion.5 = f32[32,1]{0,1:T(1,128)S(1)} fusion(f32[8,8,256,1]{2,1,0,3:T(8,128)S(1)} %bitcast.153, f32[32,8,8,256]{3,2,1,0:T(8,128)S(1)} %copy-done), kind=kOutput, calls=%fused_computation.24 | convolution fusion | flops 6291456 | bytes 2162816 | tf_op jit(solution)/shard_map/dot_general | solution.py:65
  31.3 3.7 %collective-permute-done.4 = f32[32,10,1,256]{3,0,2,1:T(8,128)S(1)} collective-permute-done((f32[32,10,1,256]{3,0,2,1:T(8,128)S(1)}, f32[32,10,1,256]{3,0,2,1:T(8,128)S(1)}, u32[]{:S(2)}, u32[]{:S(2)}) %collective-permute-start.4) | collective-permute-done | bytes 327712 | tf_op jit(solution)/shard_map/ppermute | solution.py:25
  35.0 1.5 collective-permute-done.5
  36.5 2.9 %fusion.3 = f32[32,8,8,256]{3,0,2,1:T(8,128)S(1)} fusion(f32[32,8,8,256]{3,0,2,1:T(8,128)S(1)} %copy-done.2, f32[32,10,8,256]{3,0,2,1:T(8,128)S(1)} %constant_dynamic-update-slice_fusion, f32[32,10,1,256]{3,0,2,1:T(8,128)S(1)} %collective-permute-done.5, f32[32,1,8,256]{3,0,2,1:T(8,128)S(1)} %collective-permute-done.3, ...), kind=kLoop, calls=%fused_computation.4 | loop fusion | flops 9961472 | bytes 12509184 | tf_op jit(solution)/shard_map/sub | solution.py:42
  40.7 2.9 %convolution_bitcast_fusion = f32[32,32]{1,0:T(8,128)S(1)} fusion(f32[32,8,8,256]{3,0,2,1:T(8,128)S(1)} %fusion.3, f32[32,8,8,256]{3,2,1,0:T(8,128)S(1)} %copy-done), kind=kOutput, calls=%fused_computation.19 | convolution fusion | flops 201326592 | bytes 4198400 | tf_op jit(solution)/shard_map/dot_general | solution.py:64
  43.6 40.9 %all-reduce.7 = (f32[32,1]{0,1:T(1,128)S(1)}, f32[32,32]{1,0:T(8,128)S(1)}) all-reduce(f32[32,1]{0,1:T(1,128)S(1)} %convolution_bitcast_fusion.5, f32[32,32]{1,0:T(8,128)S(1)} %convolution_bitcast_fusion), channel_id=1, replica_groups=mesh['gx'=8,'gy'=4] {'gx','gy'}, use_global_device_ids=true, to_apply=%region_3.0 | all-reduce | flops 1056 | bytes 8448 | tf_op jit(solution)/shard_map/psum | solution.py:66
  84.7 2.9 %cholesky.18 = f32[32,32]{1,0:T(8,128)S(1)} custom-call(f32[32,32]{1,0:T(8,128)S(1)} %fusion.34), custom_call_target="Cholesky" | custom-call | tf_op jit(solution)/shard_map/jit(cholesky)/cholesky | solution.py:46
  88.9 2.4 %custom-call.11 = f32[1,32,32]{1,2,0:T(8,128)S(1)} custom-call(f32[1,32,32]{2,1,0:T(8,128)S(1)} %fusion.28), custom_call_target="InvertDiagBlocksLowerTriangular" | custom-call | tf_op jit(solution)/shard_map/triangular_solve/custom-call.2 | solution.py:48
  91.7 2.7 %fusion.49 = f32[1,8,8,256]{3,0,2,1:T(1,128)S(1)} fusion(f32[32,1,1,1]{0,1,3,2:T(1,128)S(1)} %convolution_bitcast_fusion.2, f32[32,8,8,256]{3,0,2,1:T(8,128)} %copy-done.3), kind=kOutput, calls=%fused_computation.94 | convolution fusion | flops 6291456 | bytes 2162816 | tf_op jit(solution)/shard_map/dot_general | solution.py:70
  98.3 3.0 %collective-permute-done.7 = f32[1,8,256]{2,1,0:T(8,128)S(1)} collective-permute-done((f32[1,8,256]{2,1,0:T(8,128)S(1)}, f32[1,8,256]{2,1,0:T(8,128)S(1)}, u32[]{:S(2)}, u32[]{:S(2)}) %collective-permute-start.7) | collective-permute-done | bytes 8224 | tf_op jit(solution)/shard_map/ppermute | solution.py:25
  101.4 3.4 %collective-permute-start.8 = (f32[10,1,256]{2,1,0:T(1,128)S(1)}, f32[10,1,256]{2,1,0:T(1,128)S(1)}, u32[]{:S(2)}, u32[]{:S(2)}) collective-permute-start(f32[10,1,256]{2,1,0:T(1,128)S(1)} %get-tuple-element.52), channel_id=1, source_target_pairs={{0,1},{1,2},{2,3},{4,5},{5,6},{6,7},{8,9},{9,10},{10,11},{12,13},{... | collective-permute-start | bytes 30728 | tf_op jit(solution)/shard_map/ppermute | solution.py:23
  106.1 2.2 %fusion.42 = f32[1,8,8,256]{3,0,2,1:T(1,128)S(1)} fusion(f32[32,1,1,1]{0,1,3,2:T(1,128)S(1)} %convolution_bitcast_fusion.2, f32[32,8,8,256]{3,2,1,0:T(8,128)S(1)} %copy-done), kind=kOutput, calls=%fused_computation.88 | convolution fusion | flops 6291456 | bytes 2162816 | tf_op jit(solution)/shard_map/dot_general | solution.py:69
  108.4 2.0 %collective-permute-done.9 = f32[10,1,256]{2,1,0:T(1,128)S(1)} collective-permute-done((f32[10,1,256]{2,1,0:T(1,128)S(1)}, f32[10,1,256]{2,1,0:T(1,128)S(1)}, u32[]{:S(2)}, u32[]{:S(2)}) %collective-permute-start.9) | collective-permute-done | bytes 10272 | tf_op jit(solution)/shard_map/ppermute | solution.py:25
  111.3 1.7 %convolution_bitcast_fusion.4 = f32[32]{0:T(128)S(1)} fusion(f32[16384,1]{0,1:T(1,128)S(1)} %bitcast.156, f32[32,16384]{1,0:T(8,128)S(1)} %bitcast.152), kind=kOutput, calls=%fused_computation.23 | convolution fusion | flops 6291456 | bytes 2162816 | tf_op jit(solution)/shard_map/dot_general | solution.py:85
  113.0 41.7 %all-reduce.6 = (f32[32]{0:T(128)S(1)}, f32[]{:T(128)}, f32[]{:T(128)}) all-reduce(f32[32]{0:T(128)S(1)} %convolution_bitcast_fusion.4, f32[]{:T(128)} %get-tuple-element.30, f32[]{:T(128)} %get-tuple-element.29), channel_id=1, replica_groups=mesh['gx'=8,'gy'=4] {'gx','gy'}, use_global_device_ids=true, to_apply=%region_8.12 | all-reduce | flops 34 | bytes 272 | tf_op jit(solution)/shard_map/psum | solution.py:86
  155.7 2.2 %fusion.36 = f32[1,8,8,256]{3,0,2,1:T(1,128)S(1)} fusion(f32[1,32]{1,0:T(1,128)S(1)} %get-tuple-element.57, f32[32,8,8,256]{3,2,1,0:T(8,128)S(1)} %copy-done), kind=kOutput, calls=%fused_computation.81 | convolution fusion | flops 6291456 | bytes 2162816 | tf_op jit(solution)/shard_map/dot_general | solution.py:90
  (56 shorter events, 14.3 us)
Async XLA Ops:
  1.3 10.8 %copy-start.6 = (f32[3,8,8,256]{3,2,1,0:T(8,128)S(1)}, f32[3,8,8,256]{3,2,1,0:T(8,128)}, u32[]{:S(2)}) copy-start(f32[3,8,8,256]{3,2,1,0:T(8,128)} %param.16) | copy-start | bytes 589828
  1.3 17.7 %collective-permute-start = (f32[1,8,256]{2,1,0:T(8,128)S(1)}, f32[1,8,256]{2,1,0:T(8,128)S(1)}, u32[]{:S(2)}, u32[]{:S(2)}) collective-permute-start(f32[1,8,256]{2,1,0:T(8,128)S(1)} %slice_bitcast_fusion.7), channel_id=1, source_target_pairs={{0,4},{4,8},{8,12},{12,16},{16,20},{20,24},{24,28},{1,5},{5,9},{9,... | collective-permute-start | bytes 24584 | tf_op jit(solution)/shard_map/ppermute | solution.py:12
  6.7 12.3 %copy-start.1 = (f32[32,8,8,256]{3,0,2,1:T(8,128)}, f32[32,8,8,256]{3,0,2,1:T(8,128)S(1)}, u32[]{:S(2)}) copy-start(f32[32,8,8,256]{3,0,2,1:T(8,128)S(1)} %copy.11) | copy-start | bytes 6291460
  7.6 11.7 %collective-permute-start.3 = (f32[32,1,8,256]{3,0,2,1:T(8,128)}, f32[32,1,8,256]{3,0,2,1:T(8,128)S(1)}, u32[]{:S(2)}, u32[]{:S(2)}) collective-permute-start(f32[32,1,8,256]{3,0,2,1:T(8,128)} %get-tuple-element.44), channel_id=1, source_target_pairs={{0,4},{4,8},{8,12},{12,16},{16,20},{20,24},{24,28},{1,5},{5,9},{9,... | collective-permute-start | bytes 786440 | tf_op jit(solution)/shard_map/ppermute | solution.py:23
  12.1 7.1 %collective-permute-start.1 = (f32[8,1,256]{2,1,0:T(1,128)S(1)}, f32[8,1,256]{2,1,0:T(1,128)S(1)}, u32[]{:S(2)}, u32[]{:S(2)}) collective-permute-start(f32[8,1,256]{2,1,0:T(1,128)S(1)} %slice.229), channel_id=1, source_target_pairs={{0,1},{1,2},{2,3},{4,5},{5,6},{6,7},{8,9},{9,10},{10,11},{12,13},{... | collective-permute-start | bytes 24584 | tf_op jit(solution)/shard_map/ppermute | solution.py:12
  15.6 3.7 %copy-start = (f32[32,8,8,256]{3,2,1,0:T(8,128)S(1)}, f32[32,8,8,256]{3,2,1,0:T(8,128)}, u32[]{:S(2)}) copy-start(f32[32,8,8,256]{3,2,1,0:T(8,128)} %param.13) | copy-start | bytes 6291460
  15.6 6.8 %collective-permute-start.2 = (f32[32,1,8,256]{3,0,2,1:T(8,128)}, f32[32,1,8,256]{3,0,2,1:T(8,128)S(1)}, u32[]{:S(2)}, u32[]{:S(2)}) collective-permute-start(f32[32,1,8,256]{3,0,2,1:T(8,128)} %get-tuple-element.43), channel_id=1, source_target_pairs={{4,0},{8,4},{12,8},{16,12},{20,16},{24,20},{28,24},{5,1},{9,5},{13... | collective-permute-start | bytes 786440 | tf_op jit(solution)/shard_map/ppermute | solution.py:25
  19.4 9.2 %copy-start.5 = (f32[8,8,256]{2,1,0:T(8,128)S(1)}, f32[8,8,256]{2,1,0:T(8,128)}, u32[]{:S(2)}) copy-start(f32[8,8,256]{2,1,0:T(8,128)} %param.14) | copy-start | bytes 196612
  22.4 14.1 %copy-start.2 = (f32[32,8,8,256]{3,0,2,1:T(8,128)S(1)}, f32[32,8,8,256]{3,0,2,1:T(8,128)}, u32[]{:S(2)}) copy-start(f32[32,8,8,256]{3,0,2,1:T(8,128)} %copy-done.1) | copy-start | bytes 6291460
  22.4 14.1 %copy-start.4 = (f32[8,8,256]{2,1,0:T(8,128)S(1)}, f32[8,8,256]{2,1,0:T(8,128)}, u32[]{:S(2)}) copy-start(f32[8,8,256]{2,1,0:T(8,128)} %param.15) | copy-start | bytes 196612
  22.5 12.5 %collective-permute-start.4 = (f32[32,10,1,256]{3,0,2,1:T(8,128)S(1)}, f32[32,10,1,256]{3,0,2,1:T(8,128)S(1)}, u32[]{:S(2)}, u32[]{:S(2)}) collective-permute-start(f32[32,10,1,256]{3,0,2,1:T(8,128)S(1)} %get-tuple-element.39), channel_id=1, source_target_pairs={{1,0},{2,1},{3,2},{5,4},{6,5},{7,6},{9,8},{10,9},{11,10},{13,12},{... | collective-permute-start | bytes 983048 | tf_op jit(solution)/shard_map/ppermute | solution.py:25
  24.0 12.5 %collective-permute-start.5 = (f32[32,10,1,256]{3,0,2,1:T(8,128)S(1)}, f32[32,10,1,256]{3,0,2,1:T(8,128)S(1)}, u32[]{:S(2)}, u32[]{:S(2)}) collective-permute-start(f32[32,10,1,256]{3,0,2,1:T(8,128)S(1)} %get-tuple-element.40), channel_id=1, source_target_pairs={{0,1},{1,2},{2,3},{4,5},{5,6},{6,7},{8,9},{9,10},{10,11},{12,13},{... | collective-permute-start | bytes 983048 | tf_op jit(solution)/shard_map/ppermute | solution.py:23
  39.4 1.3 copy-start.3
  94.5 3.8 %collective-permute-start.6 = (f32[1,8,256]{2,1,0:T(8,128)S(1)}, f32[1,8,256]{2,1,0:T(8,128)S(1)}, u32[]{:S(2)}, u32[]{:S(2)}) collective-permute-start(f32[1,8,256]{2,1,0:T(8,128)S(1)} %get-tuple-element.54), channel_id=1, source_target_pairs={{0,4},{4,8},{8,12},{12,16},{16,20},{20,24},{24,28},{1,5},{5,9},{9,... | collective-permute-start | bytes 24584 | tf_op jit(solution)/shard_map/ppermute | solution.py:23
  95.8 5.6 %collective-permute-start.7 = (f32[1,8,256]{2,1,0:T(8,128)S(1)}, f32[1,8,256]{2,1,0:T(8,128)S(1)}, u32[]{:S(2)}, u32[]{:S(2)}) collective-permute-start(f32[1,8,256]{2,1,0:T(8,128)S(1)} %get-tuple-element.55), channel_id=1, source_target_pairs={{4,0},{8,4},{12,8},{16,12},{20,16},{24,20},{28,24},{5,1},{9,5},{13... | collective-permute-start | bytes 24584 | tf_op jit(solution)/shard_map/ppermute | solution.py:25
  101.4 7.0 %collective-permute-start.8 = (f32[10,1,256]{2,1,0:T(1,128)S(1)}, f32[10,1,256]{2,1,0:T(1,128)S(1)}, u32[]{:S(2)}, u32[]{:S(2)}) collective-permute-start(f32[10,1,256]{2,1,0:T(1,128)S(1)} %get-tuple-element.52), channel_id=1, source_target_pairs={{0,1},{1,2},{2,3},{4,5},{5,6},{6,7},{8,9},{9,10},{10,11},{12,13},{... | collective-permute-start | bytes 30728 | tf_op jit(solution)/shard_map/ppermute | solution.py:23
  104.8 5.6 %collective-permute-start.9 = (f32[10,1,256]{2,1,0:T(1,128)S(1)}, f32[10,1,256]{2,1,0:T(1,128)S(1)}, u32[]{:S(2)}, u32[]{:S(2)}) collective-permute-start(f32[10,1,256]{2,1,0:T(1,128)S(1)} %get-tuple-element.53), channel_id=1, source_target_pairs={{1,0},{2,1},{3,2},{5,4},{6,5},{7,6},{9,8},{10,9},{11,10},{13,12},{... | collective-permute-start | bytes 30728 | tf_op jit(solution)/shard_map/ppermute | solution.py:25
where the time goes:
time: 161 us
  blocking collectives  82.6 us (51%)
  starting transfers between devices  25.2 us (16%)
  matrix products  15.8 us (10%)
  other arithmetic  14.2 us (9%)
  waiting for transfers between devices  10.2 us (6%)
  local copies, waits for them, and re-layouts  9.6 us (6%)
  between operations  2.99 us (2%)
    psum x1, blocking collectives, on_device(): lax.psum((local_corr, jnp.sum(residual * direction), jnp.sum(direction *...  41.7 us
    psum x1, blocking collectives, on_device(): gram, projected = lax.psum((local_gram, local_proj), ('gx', 'gy'))  40.9 us
    ppermute x4, starting transfers between devices, padded_2(): lax.ppermute(tail, axis, [(i, (i + 1) % count) for i in range(ends)])  13.8 us
    ppermute x4, waiting for transfers between devices, padded_2(): lax.ppermute(head, axis, [((i + 1) % count, i) for i in range(ends)])  8.74 us
    ppermute x2, starting transfers between devices, shifted(): return lax.ppermute(block, axis, route)  6 us
    unnamed x18, local copies, waits for them, and re-layouts  5.48 us
    ppermute x4, starting transfers between devices, padded_2(): lax.ppermute(head, axis, [((i + 1) % count, i) for i in range(ends)])  5.43 us
    another operation x3, other arithmetic, small_solve(): lower = jnp.linalg.cholesky(matrix)  3.6 us
  transfers between devices with their start and end apart: 10, of which 4 were waited for; matrix products, arithmetic and copies ran while one was open for 9% of the time, Pallas kernels for 0%

commit v1 on v0

--- a/solution.py
+++ b/solution.py
@@ -1,9 +1,19 @@
+import functools
 import jax
 import jax.numpy as jnp
 from jax import lax
 from jax.sharding import PartitionSpec as P
 
 precise = lax.Precision.HIGHEST
+
+
+def tell_scenes(u_in, mesh_ax, mesh_name):
+    for kk in (mesh_ax, mesh_name):
+        u_in = lax.psum(u_in, axis_name=kk)
+    return u_in
+
+
+pack_seats_all = functools.partial(tell_scenes, mesh_ax="gy", mesh_name="gx")
 
 
 def shifted(block, axis, distance):
@@ -83,8 +93,8 @@
     direction_pad = padded_2(direction, (("gx", 0), ("gy", 1)), 1)
     applied_dir = flux_apply(direction_pad[None], coeff_pad, extra_diag)[0]
     local_corr = jnp.dot(flat_basis, applied_dir.reshape(-1), precision=precise)
-    correction, numerator, curvature = lax.psum(
-        (local_corr, jnp.sum(residual * direction), jnp.sum(direction * applied_dir)), ("gx", "gy")
+    correction, numerator, curvature = pack_seats_all(
+        (local_corr, jnp.sum(residual * direction), jnp.sum(direction * applied_dir))
     )
     shift_coef = small_solve(gram, correction)
     update = direction - jnp.tensordot(shift_coef, basis, axes=1, precision=precise)

time: 161 us -> 143 us (0.89)
  blocking collectives: 82.6 us -> 64.5 us
    psum x1 -> x2, blocking collectives: 41.7 us -> 23.6 us  [tell_scenes(): u_in = lax.psum(u_in, axis_name=kk)]
  transfers between devices with their start and end apart: 10 -> 10, of which waited for: 4 -> 4; matrix products, arithmetic and copies ran while one was open for 9% -> 11% of each run, Pallas kernels for 0% -> 0%
where the time goes in v1:
time: 143 us
  blocking collectives  64.5 us (45%)
  starting transfers between devices  25.2 us (18%)
  matrix products  15.8 us (11%)
  other arithmetic  14.2 us (10%)
  waiting for transfers between devices  10.2 us (7%)
  local copies, waits for them, and re-layouts  9.62 us (7%)
  between operations  2.99 us (2%)
    psum x1, blocking collectives, on_device(): gram, projected = lax.psum((local_gram, local_proj), ('gx', 'gy'))  40.9 us
    psum x2, blocking collectives, tell_scenes(): u_in = lax.psum(u_in, axis_name=kk)  23.6 us
    ppermute x4, starting transfers between devices, padded_2(): lax.ppermute(tail, axis, [(i, (i + 1) % count) for i in range(ends)])  13.8 us
    ppermute x4, waiting for transfers between devices, padded_2(): lax.ppermute(head, axis, [((i + 1) % count, i) for i in range(ends)])  8.74 us
    ppermute x2, starting transfers between devices, shifted(): return lax.ppermute(block, axis, route)  6 us
    unnamed x18, local copies, waits for them, and re-layouts  5.49 us
    ppermute x4, starting transfers between devices, padded_2(): lax.ppermute(head, axis, [((i + 1) % count, i) for i in range(ends)])  5.43 us
    another operation x3, other arithmetic, small_solve(): lower = jnp.linalg.cholesky(matrix)  3.6 us
  transfers between devices with their start and end apart: 10, of which 4 were waited for; matrix products, arithmetic and copies ran while one was open for 11% of the time, Pallas kernels for 0%

profile of v1, /device:TPU:0, one launch (start us, length us, event | category | flops | bytes accessed | tf_op | source)
XLA Modules:
  0.0 142.5 jit_solution(980513942333689519)
XLA Ops:
  1.3 2.5 %collective-permute-start = (f32[1,8,256]{2,1,0:T(8,128)S(1)}, f32[1,8,256]{2,1,0:T(8,128)S(1)}, u32[]{:S(2)}, u32[]{:S(2)}) collective-permute-start(f32[1,8,256]{2,1,0:T(8,128)S(1)} %slice_bitcast_fusion.7), channel_id=1, source_target_pairs={{0,4},{4,8},{8,12},{12,16},{16,20},{20,24},{24,28},{1,5},{5,9},{9,... | collective-permute-start | bytes 24584 | tf_op jit(solution)/shard_map/ppermute | solution.py:22
  3.9 2.8 %copy.11 = f32[32,8,8,256]{3,0,2,1:T(8,128)S(1)} copy(f32[32,8,8,256]{3,2,1,0:T(8,128)} %param.13) | data formatting | bytes 4194304 | tf_op args[0]
  7.6 4.5 %collective-permute-start.3 = (f32[32,1,8,256]{3,0,2,1:T(8,128)}, f32[32,1,8,256]{3,0,2,1:T(8,128)S(1)}, u32[]{:S(2)}, u32[]{:S(2)}) collective-permute-start(f32[32,1,8,256]{3,0,2,1:T(8,128)} %get-tuple-element.47), channel_id=1, source_target_pairs={{0,4},{4,8},{8,12},{12,16},{16,20},{20,24},{24,28},{1,5},{5,9},{9,... | collective-permute-start | bytes 786440 | tf_op jit(solution)/shard_map/ppermute | solution.py:33
  12.1 3.5 %collective-permute-start.1 = (f32[8,1,256]{2,1,0:T(1,128)S(1)}, f32[8,1,256]{2,1,0:T(1,128)S(1)}, u32[]{:S(2)}, u32[]{:S(2)}) collective-permute-start(f32[8,1,256]{2,1,0:T(1,128)S(1)} %slice.229), channel_id=1, source_target_pairs={{0,1},{1,2},{2,3},{4,5},{5,6},{6,7},{8,9},{9,10},{10,11},{12,13},{... | collective-permute-start | bytes 24584 | tf_op jit(solution)/shard_map/ppermute | solution.py:22
  17.1 1.9 %slice.236 = f32[32,8,8,255]{3,0,2,1:T(8,128)} slice(f32[32,8,8,256]{3,0,2,1:T(8,128)S(1)} %copy.11), slice={[0:32], [0:8], [0:8], [1:256]} | slice | bytes 4177920 | tf_op jit(solution)/shard_map/slice | solution.py:49
  19.4 3.0 %subtract_multiply_fusion = (f32[32,8,8,256]{3,0,2,1:T(8,128)S(1)}, f32[32,10,8,256]{3,0,2,1:T(8,128)S(1)}) fusion(f32[32,8,8,255]{3,0,2,1:T(8,128)} %slice.236, f32[8,8,256]{2,1,0:T(8,128)S(1)} %get-tuple-element.51, f32[32,8,8,256]{3,2,1,0:T(8,128)S(1)} %copy-done, f32[32,10,8,256]{3,0,2,1:T(8,128)S(1)} %constant_dynamic-update-slice_fusion.2), kind=kLoop, calls=%fused_computation.18 | loop fusion | flops 1048576 | bytes 8445952 | tf_op jit(solution)/shard_map/mul | solution.py:50
  24.0 4.6 %collective-permute-start.5 = (f32[32,10,1,256]{3,0,2,1:T(8,128)S(1)}, f32[32,10,1,256]{3,0,2,1:T(8,128)S(1)}, u32[]{:S(2)}, u32[]{:S(2)}) collective-permute-start(f32[32,10,1,256]{3,0,2,1:T(8,128)S(1)} %get-tuple-element.43), channel_id=1, source_target_pairs={{0,1},{1,2},{2,3},{4,5},{5,6},{6,7},{8,9},{9,10},{10,11},{12,13},{... | collective-permute-start | bytes 983048 | tf_op jit(solution)/shard_map/ppermute | solution.py:33
  28.6 2.8 %convolution_bitcast_fusion.5 = f32[32,1]{0,1:T(1,128)S(1)} fusion(f32[8,8,256,1]{2,1,0,3:T(8,128)S(1)} %bitcast.153, f32[32,8,8,256]{3,2,1,0:T(8,128)S(1)} %copy-done), kind=kOutput, calls=%fused_computation.24 | convolution fusion | flops 6291456 | bytes 2162816 | tf_op jit(solution)/shard_map/dot_general | solution.py:75
  31.3 3.7 %collective-permute-done.4 = f32[32,10,1,256]{3,0,2,1:T(8,128)S(1)} collective-permute-done((f32[32,10,1,256]{3,0,2,1:T(8,128)S(1)}, f32[32,10,1,256]{3,0,2,1:T(8,128)S(1)}, u32[]{:S(2)}, u32[]{:S(2)}) %collective-permute-start.4) | collective-permute-done | bytes 327712 | tf_op jit(solution)/shard_map/ppermute | solution.py:35
  35.0 1.5 %collective-permute-done.5 = f32[32,10,1,256]{3,0,2,1:T(8,128)S(1)} collective-permute-done((f32[32,10,1,256]{3,0,2,1:T(8,128)S(1)}, f32[32,10,1,256]{3,0,2,1:T(8,128)S(1)}, u32[]{:S(2)}, u32[]{:S(2)}) %collective-permute-start.5) | collective-permute-done | bytes 327712 | tf_op jit(solution)/shard_map/ppermute | solution.py:33
  36.5 2.9 %fusion.3 = f32[32,8,8,256]{3,0,2,1:T(8,128)S(1)} fusion(f32[32,8,8,256]{3,0,2,1:T(8,128)S(1)} %copy-done.2, f32[32,10,8,256]{3,0,2,1:T(8,128)S(1)} %constant_dynamic-update-slice_fusion, f32[32,10,1,256]{3,0,2,1:T(8,128)S(1)} %collective-permute-done.5, f32[32,1,8,256]{3,0,2,1:T(8,128)S(1)} %collective-permute-done.3, ...), kind=kLoop, calls=%fused_computation.4 | loop fusion | flops 9961472 | bytes 12509184 | tf_op jit(solution)/shard_map/sub | solution.py:52
  40.8 2.9 %convolution_bitcast_fusion = f32[32,32]{1,0:T(8,128)S(1)} fusion(f32[32,8,8,256]{3,0,2,1:T(8,128)S(1)} %fusion.3, f32[32,8,8,256]{3,2,1,0:T(8,128)S(1)} %copy-done), kind=kOutput, calls=%fused_computation.19 | convolution fusion | flops 201326592 | bytes 4198400 | tf_op jit(solution)/shard_map/dot_general | solution.py:74
  43.6 40.9 %all-reduce.6 = (f32[32,1]{0,1:T(1,128)S(1)}, f32[32,32]{1,0:T(8,128)S(1)}) all-reduce(f32[32,1]{0,1:T(1,128)S(1)} %convolution_bitcast_fusion.5, f32[32,32]{1,0:T(8,128)S(1)} %convolution_bitcast_fusion), channel_id=1, replica_groups=mesh['gx'=8,'gy'=4] {'gx','gy'}, use_global_device_ids=true, to_apply=%region_3.0 | all-reduce | flops 1056 | bytes 8448 | tf_op jit(solution)/shard_map/psum | solution.py:76
  84.7 2.9 %cholesky.18 = f32[32,32]{1,0:T(8,128)S(1)} custom-call(f32[32,32]{1,0:T(8,128)S(1)} %fusion.34), custom_call_target="Cholesky" | custom-call | tf_op jit(solution)/shard_map/jit(cholesky)/cholesky | solution.py:56
  88.9 2.4 %custom-call.11 = f32[1,32,32]{1,2,0:T(8,128)S(1)} custom-call(f32[1,32,32]{2,1,0:T(8,128)S(1)} %fusion.28), custom_call_target="InvertDiagBlocksLowerTriangular" | custom-call | tf_op jit(solution)/shard_map/triangular_solve/custom-call.2 | solution.py:58
  91.7 2.7 %fusion.49 = f32[1,8,8,256]{3,0,2,1:T(1,128)S(1)} fusion(f32[32,1,1,1]{0,1,3,2:T(1,128)S(1)} %convolution_bitcast_fusion.2, f32[32,8,8,256]{3,0,2,1:T(8,128)} %copy-done.3), kind=kOutput, calls=%fused_computation.94 | convolution fusion | flops 6291456 | bytes 2162816 | tf_op jit(solution)/shard_map/dot_general | solution.py:80
  98.3 3.0 %collective-permute-done.7 = f32[1,8,256]{2,1,0:T(8,128)S(1)} collective-permute-done((f32[1,8,256]{2,1,0:T(8,128)S(1)}, f32[1,8,256]{2,1,0:T(8,128)S(1)}, u32[]{:S(2)}, u32[]{:S(2)}) %collective-permute-start.7) | collective-permute-done | bytes 8224 | tf_op jit(solution)/shard_map/ppermute | solution.py:35
  101.4 3.4 %collective-permute-start.8 = (f32[10,1,256]{2,1,0:T(1,128)S(1)}, f32[10,1,256]{2,1,0:T(1,128)S(1)}, u32[]{:S(2)}, u32[]{:S(2)}) collective-permute-start(f32[10,1,256]{2,1,0:T(1,128)S(1)} %get-tuple-element.55), channel_id=1, source_target_pairs={{0,1},{1,2},{2,3},{4,5},{5,6},{6,7},{8,9},{9,10},{10,11},{12,13},{... | collective-permute-start | bytes 30728 | tf_op jit(solution)/shard_map/ppermute | solution.py:33
  106.1 2.2 %fusion.42 = f32[1,8,8,256]{3,0,2,1:T(1,128)S(1)} fusion(f32[32,1,1,1]{0,1,3,2:T(1,128)S(1)} %convolution_bitcast_fusion.2, f32[32,8,8,256]{3,2,1,0:T(8,128)S(1)} %copy-done), kind=kOutput, calls=%fused_computation.88 | convolution fusion | flops 6291456 | bytes 2162816 | tf_op jit(solution)/shard_map/dot_general | solution.py:79
  108.4 2.0 %collective-permute-done.9 = f32[10,1,256]{2,1,0:T(1,128)S(1)} collective-permute-done((f32[10,1,256]{2,1,0:T(1,128)S(1)}, f32[10,1,256]{2,1,0:T(1,128)S(1)}, u32[]{:S(2)}, u32[]{:S(2)}) %collective-permute-start.9) | collective-permute-done | bytes 10272 | tf_op jit(solution)/shard_map/ppermute | solution.py:35
  111.3 1.7 %convolution_bitcast_fusion.4 = f32[32]{0:T(128)S(1)} fusion(f32[16384,1]{0,1:T(1,128)S(1)} %bitcast.156, f32[32,16384]{1,0:T(8,128)S(1)} %bitcast.152), kind=kOutput, calls=%fused_computation.23 | convolution fusion | flops 6291456 | bytes 2162816 | tf_op jit(solution)/shard_map/dot_general | solution.py:95
  113.0 10.5 %all-reduce.8 = (f32[32]{0:T(128)S(1)}, f32[]{:T(128)}, f32[]{:T(128)}) all-reduce(f32[32]{0:T(128)S(1)} %convolution_bitcast_fusion.4, f32[]{:T(128)} %get-tuple-element.30, f32[]{:T(128)} %get-tuple-element.29), channel_id=1, replica_groups=mesh['gx'=8,'gy'=4] {'gy'}, use_global_device_ids=true, to_apply=%region_10.14 | all-reduce | flops 34 | bytes 272 | tf_op jit(solution)/shard_map/psum | solution.py:12
  123.5 13.1 %all-reduce.7 = (f32[32]{0:T(128)S(1)}, f32[]{:T(128)}, f32[]{:T(128)}) all-reduce(f32[32]{0:T(128)S(1)} %get-tuple-element.36, f32[]{:T(128)} %get-tuple-element.37, f32[]{:T(128)} %get-tuple-element.38), channel_id=1, replica_groups=mesh['gx'=8,'gy'=4] {'gx'}, use_global_device_ids=true, to_apply=%region_11.15 | all-reduce | flops 34 | bytes 272 | tf_op jit(solution)/shard_map/psum | solution.py:12
  137.6 2.2 %fusion.36 = f32[1,8,8,256]{3,0,2,1:T(1,128)S(1)} fusion(f32[1,32]{1,0:T(1,128)S(1)} %get-tuple-element.60, f32[32,8,8,256]{3,2,1,0:T(8,128)S(1)} %copy-done), kind=kOutput, calls=%fused_computation.81 | convolution fusion | flops 6291456 | bytes 2162816 | tf_op jit(solution)/shard_map/dot_general | solution.py:100
  (57 shorter events, 15.8 us)
Async XLA Ops:
  1.3 10.8 %copy-start.6 = (f32[3,8,8,256]{3,2,1,0:T(8,128)S(1)}, f32[3,8,8,256]{3,2,1,0:T(8,128)}, u32[]{:S(2)}) copy-start(f32[3,8,8,256]{3,2,1,0:T(8,128)} %param.16) | copy-start | bytes 589828
  1.3 17.7 %collective-permute-start = (f32[1,8,256]{2,1,0:T(8,128)S(1)}, f32[1,8,256]{2,1,0:T(8,128)S(1)}, u32[]{:S(2)}, u32[]{:S(2)}) collective-permute-start(f32[1,8,256]{2,1,0:T(8,128)S(1)} %slice_bitcast_fusion.7), channel_id=1, source_target_pairs={{0,4},{4,8},{8,12},{12,16},{16,20},{20,24},{24,28},{1,5},{5,9},{9,... | collective-permute-start | bytes 24584 | tf_op jit(solution)/shard_map/ppermute | solution.py:22
  6.7 12.3 %copy-start.1 = (f32[32,8,8,256]{3,0,2,1:T(8,128)}, f32[32,8,8,256]{3,0,2,1:T(8,128)S(1)}, u32[]{:S(2)}) copy-start(f32[32,8,8,256]{3,0,2,1:T(8,128)S(1)} %copy.11) | copy-start | bytes 6291460
  7.6 11.8 %collective-permute-start.3 = (f32[32,1,8,256]{3,0,2,1:T(8,128)}, f32[32,1,8,256]{3,0,2,1:T(8,128)S(1)}, u32[]{:S(2)}, u32[]{:S(2)}) collective-permute-start(f32[32,1,8,256]{3,0,2,1:T(8,128)} %get-tuple-element.47), channel_id=1, source_target_pairs={{0,4},{4,8},{8,12},{12,16},{16,20},{20,24},{24,28},{1,5},{5,9},{9,... | collective-permute-start | bytes 786440 | tf_op jit(solution)/shard_map/ppermute | solution.py:33
  12.1 7.1 %collective-permute-start.1 = (f32[8,1,256]{2,1,0:T(1,128)S(1)}, f32[8,1,256]{2,1,0:T(1,128)S(1)}, u32[]{:S(2)}, u32[]{:S(2)}) collective-permute-start(f32[8,1,256]{2,1,0:T(1,128)S(1)} %slice.229), channel_id=1, source_target_pairs={{0,1},{1,2},{2,3},{4,5},{5,6},{6,7},{8,9},{9,10},{10,11},{12,13},{... | collective-permute-start | bytes 24584 | tf_op jit(solution)/shard_map/ppermute | solution.py:22
  15.6 3.7 %copy-start = (f32[32,8,8,256]{3,2,1,0:T(8,128)S(1)}, f32[32,8,8,256]{3,2,1,0:T(8,128)}, u32[]{:S(2)}) copy-start(f32[32,8,8,256]{3,2,1,0:T(8,128)} %param.13) | copy-start | bytes 6291460
  15.6 6.8 %collective-permute-start.2 = (f32[32,1,8,256]{3,0,2,1:T(8,128)}, f32[32,1,8,256]{3,0,2,1:T(8,128)S(1)}, u32[]{:S(2)}, u32[]{:S(2)}) collective-permute-start(f32[32,1,8,256]{3,0,2,1:T(8,128)} %get-tuple-element.46), channel_id=1, source_target_pairs={{4,0},{8,4},{12,8},{16,12},{20,16},{24,20},{28,24},{5,1},{9,5},{13... | collective-permute-start | bytes 786440 | tf_op jit(solution)/shard_map/ppermute | solution.py:35
  19.4 9.2 %copy-start.5 = (f32[8,8,256]{2,1,0:T(8,128)S(1)}, f32[8,8,256]{2,1,0:T(8,128)}, u32[]{:S(2)}) copy-start(f32[8,8,256]{2,1,0:T(8,128)} %param.14) | copy-start | bytes 196612
  22.4 14.1 %copy-start.2 = (f32[32,8,8,256]{3,0,2,1:T(8,128)S(1)}, f32[32,8,8,256]{3,0,2,1:T(8,128)}, u32[]{:S(2)}) copy-start(f32[32,8,8,256]{3,0,2,1:T(8,128)} %copy-done.1) | copy-start | bytes 6291460
  22.4 14.1 %copy-start.4 = (f32[8,8,256]{2,1,0:T(8,128)S(1)}, f32[8,8,256]{2,1,0:T(8,128)}, u32[]{:S(2)}) copy-start(f32[8,8,256]{2,1,0:T(8,128)} %param.15) | copy-start | bytes 196612
  22.5 12.5 %collective-permute-start.4 = (f32[32,10,1,256]{3,0,2,1:T(8,128)S(1)}, f32[32,10,1,256]{3,0,2,1:T(8,128)S(1)}, u32[]{:S(2)}, u32[]{:S(2)}) collective-permute-start(f32[32,10,1,256]{3,0,2,1:T(8,128)S(1)} %get-tuple-element.42), channel_id=1, source_target_pairs={{1,0},{2,1},{3,2},{5,4},{6,5},{7,6},{9,8},{10,9},{11,10},{13,12},{... | collective-permute-start | bytes 983048 | tf_op jit(solution)/shard_map/ppermute | solution.py:35
  24.0 12.5 %collective-permute-start.5 = (f32[32,10,1,256]{3,0,2,1:T(8,128)S(1)}, f32[32,10,1,256]{3,0,2,1:T(8,128)S(1)}, u32[]{:S(2)}, u32[]{:S(2)}) collective-permute-start(f32[32,10,1,256]{3,0,2,1:T(8,128)S(1)} %get-tuple-element.43), channel_id=1, source_target_pairs={{0,1},{1,2},{2,3},{4,5},{5,6},{6,7},{8,9},{9,10},{10,11},{12,13},{... | collective-permute-start | bytes 983048 | tf_op jit(solution)/shard_map/ppermute | solution.py:33
  39.4 1.4 copy-start.3
  94.5 3.8 %collective-permute-start.6 = (f32[1,8,256]{2,1,0:T(8,128)S(1)}, f32[1,8,256]{2,1,0:T(8,128)S(1)}, u32[]{:S(2)}, u32[]{:S(2)}) collective-permute-start(f32[1,8,256]{2,1,0:T(8,128)S(1)} %get-tuple-element.57), channel_id=1, source_target_pairs={{0,4},{4,8},{8,12},{12,16},{16,20},{20,24},{24,28},{1,5},{5,9},{9,... | collective-permute-start | bytes 24584 | tf_op jit(solution)/shard_map/ppermute | solution.py:33
  95.8 5.6 %collective-permute-start.7 = (f32[1,8,256]{2,1,0:T(8,128)S(1)}, f32[1,8,256]{2,1,0:T(8,128)S(1)}, u32[]{:S(2)}, u32[]{:S(2)}) collective-permute-start(f32[1,8,256]{2,1,0:T(8,128)S(1)} %get-tuple-element.58), channel_id=1, source_target_pairs={{4,0},{8,4},{12,8},{16,12},{20,16},{24,20},{28,24},{5,1},{9,5},{13... | collective-permute-start | bytes 24584 | tf_op jit(solution)/shard_map/ppermute | solution.py:35
  101.4 7.0 %collective-permute-start.8 = (f32[10,1,256]{2,1,0:T(1,128)S(1)}, f32[10,1,256]{2,1,0:T(1,128)S(1)}, u32[]{:S(2)}, u32[]{:S(2)}) collective-permute-start(f32[10,1,256]{2,1,0:T(1,128)S(1)} %get-tuple-element.55), channel_id=1, source_target_pairs={{0,1},{1,2},{2,3},{4,5},{5,6},{6,7},{8,9},{9,10},{10,11},{12,13},{... | collective-permute-start | bytes 30728 | tf_op jit(solution)/shard_map/ppermute | solution.py:33
  104.8 5.6 %collective-permute-start.9 = (f32[10,1,256]{2,1,0:T(1,128)S(1)}, f32[10,1,256]{2,1,0:T(1,128)S(1)}, u32[]{:S(2)}, u32[]{:S(2)}) collective-permute-start(f32[10,1,256]{2,1,0:T(1,128)S(1)} %get-tuple-element.56), channel_id=1, source_target_pairs={{1,0},{2,1},{3,2},{5,4},{6,5},{7,6},{9,8},{10,9},{11,10},{13,12},{... | collective-permute-start | bytes 30728 | tf_op jit(solution)/shard_map/ppermute | solution.py:35
